TPU v7x, 128 devices: a whole 4x4x4 slice. The times are simulated.
128 devices in a mesh: scan: 16 (over z, y), row: 8 (over x, core).
Axes of the slice: x: 4, y: 4, z: 4, core: 2. Of those that a mesh axis runs over, the one named last changes fastest.
Arguments:
- raw_planes: float32 [32, 6, 128, 1024], P('scan', None, 'row'), may hold values from 0 to 4
- shear_tiles: int32 [32], P('scan'), may hold values from 0 to 5, as said below
- axial_kernel: float32 [64], replicated, may hold values from 0.05 to 1
- column_kernel: float32 [31], replicated, may hold values from 0.05 to 1
- row_kernel: float32 [31], replicated, may hold values from 0.05 to 1
Outputs:
- estimate: float32 [32, 16, 128, 1024], P(None, 'scan', 'row')
Inputs may be any that keep to these rules, and one draw needn't show every extreme that they name: `shear_tiles`: plane p has a shear within one tile of p * 5 // 31; the first plane has 0 and the last 5.
All inputs are finite; a program needn't handle non-finite values.
Results may differ from a plain program's by a relative error of at most 0.0003.
Values sent between devices are 32-bit elements; how exact they have to be, the bound alone decides.
A program may use at most 128 MiB of HBM per device.

v0:
```python
import jax
import jax.numpy as jnp
from jax import lax
from jax.sharding import PartitionSpec as P

TILES_DEV = 1
ITERS = 2


background_level = 0.5


def normalized(kernel):
    return kernel / jnp.sum(kernel)


def band_matrix(kernel, extent):
    length = kernel.shape[0]
    centre = length // 2
    indices = jnp.arange(extent, dtype=jnp.int32)
    offset = indices[None, :] - indices[:, None] + centre
    inside = (offset >= 0) & (offset < length)
    return jnp.where(inside, kernel[jnp.clip(offset, 0, length - 1)], 0.0)


def shifted_sum(volume, kernel, centre, axis):
    length = kernel.shape[0]
    extent = volume.shape[axis]
    widths = [(0, 0)] * volume.ndim
    widths[axis] = (centre, length - 1 - centre)
    padded = jnp.pad(volume, widths)
    summed = jnp.zeros_like(volume)
    for tap in range(length):
        summed = summed + kernel[tap] * lax.slice_in_dim(padded, tap, tap + extent, axis=axis)
    return summed


def spread_planes(tiles_in, shear_tiles, total):

    def place_plane(one_plane, offset):
        empty_slab = jnp.zeros((total,) + one_plane.shape[1:], one_plane.dtype)
        anchor = jnp.zeros((), jnp.int32)
        return lax.dynamic_update_slice(empty_slab, one_plane, (offset, anchor, anchor))

    return jax.vmap(place_plane)(tiles_in, shear_tiles)


def axial_apply(matrix, volume):
    flattened = volume.reshape(volume.shape[0], -1)
    result = jnp.dot(matrix, flattened, precision=lax.Precision.HIGHEST)
    return result.reshape(volume.shape)


def rows_layout(volume):
    result = lax.all_to_all(
        lax.all_to_all(volume, "scan", split_axis=0, concat_axis=1, tiled=True),
        "row",
        split_axis=3,
        concat_axis=2,
        tiled=True,
    )
    return result


def pencil_layout(volume):
    result = lax.all_to_all(
        lax.all_to_all(volume, "scan", split_axis=1, concat_axis=0, tiled=True),
        "row",
        split_axis=2,
        concat_axis=3,
        tiled=True,
    )
    return result


def shards(raw_planes, shear_tiles, axial_kernel, column_kernel, row_kernel):
    scan_count = lax.axis_size("scan")
    out_count = TILES_DEV * scan_count
    axial = normalized(axial_kernel)
    across = normalized(column_kernel)
    down = normalized(row_kernel)
    lateral_len = across.shape[0]
    lateral_centre = lateral_len // 2
    back_centre = lateral_len - 1 - lateral_centre
    spread = spread_planes(raw_planes, shear_tiles, out_count)
    data_pencils = lax.all_to_all(spread, "scan", split_axis=1, concat_axis=0, tiled=True)
    data_rows = rows_layout(data_pencils)
    row_shape = data_rows.shape
    data_flat = data_rows.reshape(row_shape[0], row_shape[1] * row_shape[2], row_shape[3])
    axial_band = band_matrix(axial, data_pencils.shape[0])
    estimate = data_pencils + 1.0
    for iteration in range(ITERS):
        blurred = axial_apply(axial_band, estimate)
        blurred = shifted_sum(blurred, across, lateral_centre, 3)
        blurred_rows = rows_layout(blurred)
        flattened = blurred_rows.reshape(data_flat.shape)
        flattened = shifted_sum(flattened, down, lateral_centre, 1)
        quotient = data_flat / (flattened + background_level)
        quotient = shifted_sum(quotient, down[::-1], back_centre, 1)
        correction = pencil_layout(quotient.reshape(row_shape))
        correction = shifted_sum(correction, across[::-1], back_centre, 3)
        correction = axial_apply(axial_band.T, correction)
        estimate = estimate * correction
    return estimate


def solution(mesh):
    return jax.shard_map(
        shards,
        mesh=mesh,
        in_specs=(P("scan", None, "row", None), P("scan"), P(), P(), P()),
        out_specs=P(None, "scan", "row", None),
        check_vma=False,
    )
```

profile of v0, /device:TPU:32, one launch (start us, length us, event | category | flops | bytes accessed | tf_op | source)
XLA Modules:
  0.0 923.6 jit_solution(2786880016588994488)
XLA Ops:
  3.2 17.7 %while.1 = (s32[]{:T(128)}, f32[2,16,16,1024]{3,2,0,1:T(8,128)}, s32[2,4]{1,0:T(2,128)S(1)}, f32[2,6,16,1024]{3,2,1,0:T(8,128)S(1)}, s32[]{:T(128)}, /*index=5*/s32[4]{0:T(128)S(1)}) while((s32[]{:T(128)}, f32[2,16,16,1024]{3,2,0,1:T(8,128)}, s32[2,4]{1,0:T(2,128)S(1)}, f32[2,6,16,1024]{3,2,1,0:T(8,128)S(1)}, s32[]{:T(128)}, ...), condition=%wide.while_cond, body=%wide.while_body.sunk | while | flops 98333 | bytes 1968306 | solution.py:43
  3.8 3.2 and_reduce_fusion.2
  9.3 2.7 bitcast_dynamic-update-slice_fusion.2
  12.6 3.2 and_reduce_fusion.2
  18.1 2.7 bitcast_dynamic-update-slice_fusion.2
  20.8 8.2 all-to-all-start
  31.1 6.6 gather_fusion
  39.9 19.6 %all-to-all-done = f32[2,16,16,1024]{3,2,0,1:T(8,128)} async-done(((f32[2,16,16,1024]{3,2,0,1:T(8,128)}), f32[2,16,16,1024]{3,2,0,1:T(8,128)}, u32[]{:S(2)}, u32[]{:S(2)}) %all-to-all-start) | async-done | bytes 2097184 | tf_op jit(solution)/shard_map/all_to_all | solution.py:86
  65.7 36.0 %fusion.53 = f32[32,1,16,1024]{3,2,1,0:T(8,128)S(1)} fusion(f32[32,1,16,1024]{3,2,1,0:T(8,128)S(1)} %bitcast.299, f32[]{:T(128)} %bitcast.50, f32[]{:T(128)} %bitcast.49, f32[]{:T(128)} %bitcast.48, f32[]{:T(128)} %bitcast.47, f32[]{:T(128)} %bitcast.46, f32[]{:T(128)} %bitcast.45, f32[]{:T(128)} %bitcast.44, f32[]{:T(128)} %bitcast.43, f32[]{:T(128)} %bitcast.42, ...), kind=kLoop, calls=%fused_computation.179 | loop fusion | flops 31981568 | bytes 4194428 | tf_op jit(solution)/shard_map/add | solution.py:34
  101.7 30.3 %all_to_all.189 = f32[32,1,16,1024]{3,2,1,0:T(8,128)} all-to-all(f32[32,1,16,1024]{3,2,1,0:T(8,128)S(1)} %fusion.53), channel_id=1, replica_groups=mesh['scan'=16,'row'=8] {'scan'}, dimensions={0} | all-to-all | bytes 4194304 | tf_op jit(solution)/shard_map/all_to_all | solution.py:56
  131.9 6.5 all-to-all-start.1
  138.5 21.4 %copy.97 = f32[2,16,16,1024]{2,0,1,3:T(2,128)} copy(f32[2,16,16,1024]{3,2,0,1:T(8,128)} %bitcast.293) | data formatting | bytes 4194304 | tf_op jit(solution)/shard_map/all_to_all | solution.py:56
  159.9 24.7 %reshape.188 = f32[8,1,65536]{2,1,0:T(1,128)} reshape(f32[1024,16,2,16]{3,2,1,0:T(2,128)} %bitcast.282) | data formatting | bytes 4194304
  184.6 4.4 all-to-all-start.4
  189.0 13.6 %copy.92 = f32[16,2,1,16,1024]{3,0,1,4,2:T(8,128)} copy(f32[16,2,1,16,1024]{4,3,1,0,2:T(8,128)S(1)} %bitcast.292) | data formatting | bytes 4194304 | tf_op jit(solution)/shard_map/all_to_all | solution.py:56
  202.6 11.6 %bitcast_bitcast_fusion = f32[1024,2,16,16]{3,2,1,0:T(8,128)} fusion(f32[16,2,1,16,1024]{3,0,1,4,2:T(8,128)} %copy.92), kind=kLoop, calls=%fused_computation.512 | loop fusion | bytes 4194304
  214.2 11.6 %reshape.186 = f32[8,1,65536]{2,1,0:T(1,128)} reshape(f32[1024,2,16,16]{3,2,1,0:T(8,128)} %bitcast_bitcast_fusion) | data formatting | bytes 4194304
  225.8 4.9 all-to-all-start.2
  235.5 7.3 reduce.3
  242.7 28.4 %reshape.189 = f32[1024,16,2,16]{3,2,1,0:T(2,128)} reshape(f32[8,65536]{1,0:T(8,128)S(1)} %reduce.3) | data formatting | bytes 4194304
  271.1 21.8 %copy.130 = f32[2,16,16,8,128]{4,2,3,1,0:T(8,128)} copy(f32[2,16,16,8,128]{2,0,1,4,3:T(2,128)} %bitcast.283) | data formatting | bytes 4194304 | tf_op jit(solution)/shard_map/all_to_all | solution.py:55
  293.0 7.3 reduce.2
  300.2 11.3 %reshape.187 = f32[1024,2,16,16]{3,2,1,0:T(8,128)} reshape(f32[8,65536]{1,0:T(8,128)S(1)} %reduce.2) | data formatting | bytes 4194304
  311.5 9.8 %copy.94 = f32[2,16,8,16,128]{4,3,2,1,0:T(8,128)S(1)} copy(f32[2,16,8,16,128]{3,1,0,4,2:T(8,128)} %bitcast.284) | data formatting | bytes 4194304 | tf_op jit(solution)/shard_map/all_to_all | solution.py:55
  321.3 57.8 %bitcast_divide_fusion.1 = f32[2,2048,128]{2,1,0:T(8,128)S(1)} fusion(f32[2,16,8,16,128]{4,3,2,1,0:T(8,128)S(1)} %copy.94, f32[2,2048,128]{2,1,0:T(8,128)} %bitcast.291, f32[]{:T(128)} %bitcast.88, f32[]{:T(128)} %bitcast.87, f32[]{:T(128)} %bitcast.86, f32[]{:T(128)} %bitcast.85, f32[]{:T(128)} %bitcast.84, f32[]{:T(128)} %bitcast.83, f32[]{:T(128)} %bitcast.82, ...), kind=kLoop, calls=%fused_computation.373 | loop fusion | flops 33030144 | bytes 6291580 | tf_op jit(solution)/shard_map/div | solution.py:98
  379.1 27.4 %multiply_add_fusion.1 = f32[2,2048,128]{2,1,0:T(8,128)S(1)} fusion(f32[2,2048,128]{2,1,0:T(8,128)S(1)} %bitcast_divide_fusion.1, f32[]{:T(128)} %bitcast.118, f32[]{:T(128)} %bitcast.117, f32[]{:T(128)} %bitcast.116, f32[]{:T(128)} %bitcast.115, f32[]{:T(128)} %bitcast.114, f32[]{:T(128)} %bitcast.113, f32[]{:T(128)} %bitcast.112, f32[]{:T(128)} %bitcast.111, ...), kind=kLoop, calls=%fused_computation.430 | loop fusion | flops 31981568 | bytes 4194428 | tf_op jit(solution)/shard_map/add | solution.py:34
  406.8 33.7 %all_to_all.190 = f32[2,16,128,128]{3,2,0,1:T(8,128)S(1)} all-to-all(f32[2,16,128,128]{3,2,0,1:T(8,128)S(1)} %copy.100), channel_id=1, replica_groups=mesh['scan'=16,'row'=8] {'scan'}, dimensions={1} | all-to-all | bytes 4194304 | tf_op jit(solution)/shard_map/all_to_all | solution.py:67
  440.4 2.5 copy.101
  443.0 4.4 all-to-all-start.6
  448.8 25.8 %all-to-all-done.6 = f32[32,1,128,128]{3,0,1,2:T(8,128)} async-done(((f32[32,1,128,128]{3,0,1,2:T(8,128)}), f32[32,1,128,128]{3,0,1,2:T(8,128)}, u32[]{:S(2)}, u32[]{:S(2)}) %all-to-all-start.6) | async-done | bytes 2097184 | tf_op jit(solution)/shard_map/all_to_all | solution.py:66
  474.6 2.8 copy.102
  478.8 36.3 %fusion.113 = f32[32,1,16,1024]{3,2,1,0:T(8,128)S(1)} fusion(f32[32,1,16,1024]{3,2,1,0:T(8,128)S(1)} %copy.104, f32[]{:T(128)} %bitcast.155, f32[]{:T(128)} %bitcast.154, f32[]{:T(128)} %bitcast.153, f32[]{:T(128)} %bitcast.152, f32[]{:T(128)} %bitcast.151, f32[]{:T(128)} %bitcast.150, f32[]{:T(128)} %bitcast.149, f32[]{:T(128)} %bitcast.148, f32[]{:T(128)} %bitcast.147, ...), kind=kLoop, calls=%fused_computation.239 | loop fusion | flops 31981568 | bytes 4194428 | tf_op jit(solution)/shard_map/add | solution.py:34
  515.1 4.1 copy_multiply_fusion
  523.7 36.0 %fusion.173 = f32[32,1,16,1024]{3,2,1,0:T(8,128)S(1)} fusion(f32[32,1,16,1024]{3,2,1,0:T(8,128)S(1)} %bitcast.297, f32[]{:T(128)} %bitcast.50, f32[]{:T(128)} %bitcast.49, f32[]{:T(128)} %bitcast.48, f32[]{:T(128)} %bitcast.47, f32[]{:T(128)} %bitcast.46, f32[]{:T(128)} %bitcast.45, f32[]{:T(128)} %bitcast.44, f32[]{:T(128)} %bitcast.43, f32[]{:T(128)} %bitcast.42, ...), kind=kLoop, calls=%fused_computation.299 | loop fusion | flops 31981568 | bytes 4194428 | tf_op jit(solution)/shard_map/add | solution.py:34
  559.7 31.7 %all_to_all.191 = f32[32,1,16,1024]{3,2,1,0:T(8,128)} all-to-all(f32[32,1,16,1024]{3,2,1,0:T(8,128)S(1)} %fusion.173), channel_id=1, replica_groups=mesh['scan'=16,'row'=8] {'scan'}, dimensions={0} | all-to-all | bytes 4194304 | tf_op jit(solution)/shard_map/all_to_all | solution.py:56
  591.4 21.4 %copy.111 = f32[2,16,16,1024]{2,0,1,3:T(2,128)} copy(f32[2,16,16,1024]{3,2,0,1:T(8,128)} %bitcast.294) | data formatting | bytes 4194304 | tf_op jit(solution)/shard_map/all_to_all | solution.py:56
  612.8 24.7 %reshape.190 = f32[8,1,65536]{2,1,0:T(1,128)} reshape(f32[1024,16,2,16]{3,2,1,0:T(2,128)} %bitcast.285) | data formatting | bytes 4194304
  637.5 31.8 %all_to_all.192 = f32[8,1,65536]{2,1,0:T(1,128)} all-to-all(f32[8,1,65536]{2,1,0:T(1,128)} %reshape.190), channel_id=1, replica_groups=mesh['scan'=16,'row'=8] {'row'}, dimensions={0} | all-to-all | bytes 4194304 | tf_op jit(solution)/shard_map/all_to_all | solution.py:55
  669.4 8.6 reduce.4
  678.0 31.8 %reshape.191 = f32[1024,16,2,16]{3,2,1,0:T(2,128)} reshape(f32[8,65536]{1,0:T(8,128)} %reduce.4) | data formatting | bytes 4194304
  709.7 21.6 %copy.133 = f32[2,16,16,8,128]{4,2,3,1,0:T(8,128)} copy(f32[2,16,16,8,128]{2,0,1,4,3:T(2,128)} %bitcast.286) | data formatting | bytes 4194304 | tf_op jit(solution)/shard_map/all_to_all | solution.py:55
  731.4 57.3 %bitcast_divide_fusion = f32[2,2048,128]{2,1,0:T(8,128)S(1)} fusion(f32[2,16,8,16,128]{4,3,2,1,0:T(8,128)S(1)} %copy.94, f32[2,2048,128]{2,1,0:T(8,128)} %bitcast.290, f32[]{:T(128)} %bitcast.88, f32[]{:T(128)} %bitcast.87, f32[]{:T(128)} %bitcast.86, f32[]{:T(128)} %bitcast.85, f32[]{:T(128)} %bitcast.84, f32[]{:T(128)} %bitcast.83, f32[]{:T(128)} %bitcast.82, ...), kind=kLoop, calls=%fused_computation.372 | loop fusion | flops 33030144 | bytes 6291580 | tf_op jit(solution)/shard_map/div | solution.py:98
  788.7 27.6 %multiply_add_fusion = f32[2,2048,128]{2,1,0:T(8,128)S(1)} fusion(f32[2,2048,128]{2,1,0:T(8,128)S(1)} %bitcast_divide_fusion, f32[]{:T(128)} %bitcast.118, f32[]{:T(128)} %bitcast.117, f32[]{:T(128)} %bitcast.116, f32[]{:T(128)} %bitcast.115, f32[]{:T(128)} %bitcast.114, f32[]{:T(128)} %bitcast.113, f32[]{:T(128)} %bitcast.112, f32[]{:T(128)} %bitcast.111, ...), kind=kLoop, calls=%fused_computation.377 | loop fusion | flops 31981568 | bytes 4194428 | tf_op jit(solution)/shard_map/add | solution.py:34
  816.5 31.2 %all_to_all.193 = f32[2,16,128,128]{3,2,0,1:T(8,128)S(1)} all-to-all(f32[2,16,128,128]{3,2,0,1:T(8,128)S(1)} %copy.114), channel_id=1, replica_groups=mesh['scan'=16,'row'=8] {'scan'}, dimensions={1} | all-to-all | bytes 4194304 | tf_op jit(solution)/shard_map/all_to_all | solution.py:67
  848.9 30.0 %all_to_all.194 = f32[32,1,128,128]{3,0,1,2:T(8,128)S(1)} all-to-all(f32[32,1,128,128]{3,0,1,2:T(8,128)S(1)} %copy.115), channel_id=1, replica_groups=mesh['scan'=16,'row'=8] {'row'}, dimensions={2} | all-to-all | bytes 4194304 | tf_op jit(solution)/shard_map/all_to_all | solution.py:66
  881.5 36.1 %fusion.233 = f32[32,1,16,1024]{3,2,1,0:T(8,128)S(1)} fusion(f32[32,1,16,1024]{3,2,1,0:T(8,128)S(1)} %copy.118, f32[]{:T(128)} %bitcast.155, f32[]{:T(128)} %bitcast.154, f32[]{:T(128)} %bitcast.153, f32[]{:T(128)} %bitcast.152, f32[]{:T(128)} %bitcast.151, f32[]{:T(128)} %bitcast.150, f32[]{:T(128)} %bitcast.149, f32[]{:T(128)} %bitcast.148, f32[]{:T(128)} %bitcast.147, ...), kind=kLoop, calls=%fused_computation.359 | loop fusion | flops 31981568 | bytes 4194428 | tf_op jit(solution)/shard_map/add | solution.py:34
  917.6 3.1 multiply_bitcast_fusion
  920.7 2.5 copy.122
  (69 shorter events, 35.6 us)
Async XLA Ops:
  0.0 3.2 copy-start.5
  0.0 3.2 copy-start.4
  20.8 8.2 copy-start.6
  20.8 9.0 copy-start.8
  20.8 38.7 %all-to-all-start = ((f32[2,16,16,1024]{3,2,0,1:T(8,128)}), f32[2,16,16,1024]{3,2,0,1:T(8,128)}, u32[]{:S(2)}, u32[]{:S(2)}) async-start(f32[2,16,16,1024]{3,2,0,1:T(8,128)} %get-tuple-element.10), calls=%async_computation | async-start | bytes 4194304 | tf_op jit(solution)/shard_map/all_to_all | solution.py:86
  61.3 1.3 copy-start.2
  131.9 52.7 %all-to-all-start.1 = ((f32[32,1,16,1024]{3,2,1,0:T(8,128)}), f32[32,1,16,1024]{3,2,1,0:T(8,128)S(1)}, u32[]{:S(2)}, u32[]{:S(2)}) async-start(f32[32,1,16,1024]{3,2,1,0:T(8,128)} %bitcast.9), calls=%async_computation.1 | async-start | bytes 4194304 | tf_op jit(solution)/shard_map/all_to_all | solution.py:56
  184.6 41.1 %all-to-all-start.4 = ((f32[8,1,65536]{2,1,0:T(1,128)}), f32[8,1,65536]{2,1,0:T(1,128)}, u32[]{:S(2)}, u32[]{:S(2)}) async-start(f32[8,1,65536]{2,1,0:T(1,128)} %reshape.188), calls=%async_computation.4 | async-start | bytes 4194304 | tf_op jit(solution)/shard_map/all_to_all | solution.py:55
  225.8 4.9 copy-start.7
  225.8 67.2 %all-to-all-start.2 = ((f32[8,1,65536]{2,1,0:T(1,128)}), f32[8,1,65536]{2,1,0:T(1,128)}, u32[]{:S(2)}, u32[]{:S(2)}) async-start(f32[8,1,65536]{2,1,0:T(1,128)} %reshape.186), calls=%async_computation.2 | async-start | bytes 4194304 | tf_op jit(solution)/shard_map/all_to_all | solution.py:55
  443.0 31.6 %all-to-all-start.6 = ((f32[32,1,128,128]{3,0,1,2:T(8,128)}), f32[32,1,128,128]{3,0,1,2:T(8,128)}, u32[]{:S(2)}, u32[]{:S(2)}) async-start(f32[32,1,128,128]{3,0,1,2:T(8,128)} %copy.101), calls=%async_computation.6 | async-start | bytes 4194304 | tf_op jit(solution)/shard_map/all_to_all | solution.py:66
  478.8 36.3 %copy-start.3 = (f32[16,2,1,16,1024]{4,3,1,0,2:T(8,128)S(1)}, f32[16,2,1,16,1024]{4,3,1,0,2:T(8,128)}, u32[]{:S(2)}) copy-start(f32[16,2,1,16,1024]{4,3,1,0,2:T(8,128)} %copy-done.2) | copy-start | bytes 6291460
  519.3 1.3 copy-start
  881.4 36.2 %copy-start.1 = (f32[32,16,1024]{2,0,1:T(8,128)S(1)}, f32[32,16,1024]{2,0,1:T(8,128)}, u32[]{:S(2)}) copy-start(f32[32,16,1024]{2,0,1:T(8,128)} %copy-done) | copy-start | bytes 6291460
where the time goes:
time: 942 us; the launch traced here: 924 us
  other arithmetic  357 us (38%)
  local copies, waits for them, and re-layouts  293 us (31%)
  blocking collectives  189 us (20%)
  waiting for transfers between devices  45.4 us (5%)
  starting transfers between devices  28.3 us (3%)
  matrix products  11 us (1%)
    add x6, other arithmetic, shifted_sum(): summed + kernel[tap] * lax.slice_in_dim(padded, tap, tap + extent, axis=a...  199 us
    unnamed x30, local copies, waits for them, and re-layouts  149 us
    div x2, other arithmetic, shards(): quotient = data_flat / (flattened + background_level)  115 us
    all_to_all x2, blocking collectives, pencil_layout(): lax.all_to_all(volume, 'scan', split_axis=1, concat_axis=0, tiled=True)  64.8 us
    all_to_all x2, blocking collectives, rows_layout(): lax.all_to_all(volume, 'scan', split_axis=0, concat_axis=1, tiled=True)  62 us
    all_to_all x3, local copies, waits for them, and re-layouts, rows_layout(): lax.all_to_all(volume, 'scan', split_axis=0, concat_axis=1, tiled=True)  56.4 us
    all_to_all x4, local copies, waits for them, and re-layouts, rows_layout(): lax.all_to_all(lax.all_to_all(volume, 'scan', split_axis=0, concat_axis=1...  53.8 us
    all_to_all x1, blocking collectives, rows_layout(): lax.all_to_all(lax.all_to_all(volume, 'scan', split_axis=0, concat_axis=1...  31.8 us
  transfers between devices with their start and end apart: 5, of which 2 were waited for; matrix products, arithmetic and copies ran while one was open for 17% of the time, Pallas kernels for 0%

commit v1 on v0

v1 whole, which is shorter than its diff:
```python
import jax
import jax.numpy as jnp
from jax import lax
from jax.experimental import pallas as pl
from jax.experimental.pallas import tpu as pltpu
from jax.sharding import PartitionSpec as P

PLANES = 32
TILES = 6
WINDOW = 8
LAST_TILE = 10
ROWS = 64
COLS = 256
HALO = 16
ITERS = 2
BACKGROUND = 0.5
F32 = jnp.float32
BF16 = jnp.bfloat16
MESH = pl.DeviceIdType.MESH
UP, DOWN, LEFT, RIGHT, LEFT_UP, LEFT_DOWN, RIGHT_UP, RIGHT_DOWN = range(8)


def split(value):
    high = value.astype(BF16)
    low = (value - high.astype(F32)).astype(BF16)
    return high, low


def dot(a, b):
    return jnp.dot(a, b, preferred_element_type=F32)


def dot3(a, b):
    return dot(a[0], b[0]) + (dot(a[0], b[1]) + dot(a[1], b[0]))


def iota(shape, axis):
    return lax.broadcasted_iota(jnp.int32, shape, axis)


def pick(taps, count, index):
    value = jnp.zeros(index.shape, F32)
    for tap in range(count):
        value = jnp.where(index == tap, taps[tap], value)
    return value


def plane_base(plane):
    return (plane * 5) // 31


def body(raw, shear, ax_s, co_s, ro_s, ax_v, co_v, ro_v, out,
         win, data, est, quo, mid, up, down, left, right, send_left, send_right,
         band_d, band_w, band_h, band_a, strips,
         d_send, d_recv, e_send, e_recv, t_send, t_recv):
    scan = lax.axis_index("scan")
    row = lax.axis_index("row")
    x = row // 2
    core = row % 2
    block = 2 * scan + core

    for n in range(2):
        delta = shear[n] - plane_base(2 * scan + n)
        for k in range(WINDOW):
            zero = jnp.zeros(raw.shape[2:], F32)
            early = raw[n, k] if k < TILES else zero
            level = raw[n, k - 1] if 1 <= k <= TILES else zero
            late = raw[n, k - 2] if k >= 2 else zero
            win[n, k] = jnp.where(delta == 0, level, jnp.where(delta < 0, early, late))

    def deskew_copies(n, k, cb):
        plane = 2 * scan + n
        tile = plane_base(plane) - 1 + k
        half = x // 2
        offset = 32 * (x % 2) + 16 * core
        source = win.at[n, k, :, pl.ds(256 * cb, 256)]
        target = data.at[plane, pl.ds(pl.multiple_of(offset, 16), 16), :]
        real = jnp.logical_and(tile >= 0, tile <= LAST_TILE)
        mine = jnp.logical_and(tile == scan, jnp.logical_and(cb == x, half == core))
        remote = pltpu.make_async_remote_copy(
            src_ref=source, dst_ref=target, send_sem=d_send.at[n, k, cb], recv_sem=d_recv.at[plane],
            device_id=(tile, 2 * cb + half), device_id_type=MESH)
        local = pltpu.make_async_copy(source, target, d_recv.at[plane])
        return jnp.logical_and(real, mine), local, jnp.logical_and(real, jnp.logical_not(mine)), remote

    for n in range(2):
        for k in range(WINDOW):
            for cb in range(4):
                is_local, local, is_remote, remote = deskew_copies(n, k, cb)
                pl.when(is_local)(local.start)
                pl.when(is_remote)(remote.start)

    for way in range(2):
        sign = 1 if way == 0 else -1
        total = jnp.sum(ro_v[...], axis=1, keepdims=True)
        shape = (ROWS, ROWS + 2 * HALO)
        step = iota(shape, 1) - HALO - iota(shape, 0)
        high, low = split(pick(ro_s, 31, sign * step + 15) / total)
        band_d[way, 0], band_d[way, 1] = high, low

        total = jnp.sum(co_v[...], axis=1, keepdims=True)
        @pl.loop(0, 16)
        def _(b):
            shape = (16, COLS)
            start = pl.multiple_of(b * 16, 16)
            step = start + iota(shape, 0) - iota(shape, 1)
            high, low = split(pick(co_s, 31, sign * step + 15) / total)
            band_w[way, 0, pl.ds(start, 16), :] = high
            band_w[way, 1, pl.ds(start, 16), :] = low
        shape = (16, COLS)
        step = iota(shape, 0) - HALO - iota(shape, 1)
        left_band = split(pick(co_s, 31, sign * step + 15) / total)
        step = iota(shape, 0) + COLS - iota(shape, 1)
        right_band = split(pick(co_s, 31, sign * step + 15) / total)
        for part in range(2):
            band_h[way, part] = jnp.zeros((8, 2 * 128, COLS), BF16)
            for g in range(8):
                slot = 16 * ((g + 7) % 8)
                band_h[way, part, g, slot:slot + 16, :] = left_band[part]
                slot = 128 + 16 * g
                band_h[way, part, g, slot:slot + 16, :] = right_band[part]

        total = jnp.sum(ax_v[...], axis=1, keepdims=True)
        @pl.loop(0, 16)
        def _(b):
            shape = (16, 256)
            start = pl.multiple_of(b * 16, 16)
            i = start + iota(shape, 0)
            j = iota(shape, 1)
            step = jnp.where(i % 8 == j % 8, j // 8 - i // 8, -100)
            if way == 0:
                index = step + 32
            else:
                index = jnp.where(step > -50, 32 - step, -1)
            high, low = split(pick(ax_s, 64, index) / total)
            band_a[way, 0, pl.ds(start, 16), :] = high
            band_a[way, 1, pl.ds(start, 16), :] = low

    @pl.loop(0, PLANES)
    def _(plane):
        base = plane_base(plane)
        here = jnp.logical_and(jnp.logical_and(scan >= base - 1, scan <= base + 6), scan <= LAST_TILE)
        @pl.when(here)
        def _():
            pltpu.make_async_copy(data.at[plane], data.at[plane], d_recv.at[plane]).wait()
        @pl.when(jnp.logical_not(here))
        def _():
            data[plane] = jnp.zeros((ROWS, COLS), F32)

    @pl.loop(0, PLANES)
    def _(plane):
        est[plane] = data[plane] + 1.0

    lane = iota((ROWS, 128), 1)

    def exchange(e, volume):
        def place(d_block, d_x):
            other = block + d_block
            return (other // 2, 2 * (x + d_x) + other % 2)

        def copy(way, source, target, d_block, d_x):
            exists = jnp.logical_and(jnp.logical_and(block + d_block >= 0, block + d_block < 32),
                                     jnp.logical_and(x + d_x >= 0, x + d_x < 4))
            comes = jnp.logical_and(jnp.logical_and(block - d_block >= 0, block - d_block < 32),
                                    jnp.logical_and(x - d_x >= 0, x - d_x < 4))
            return exists, comes, target, pltpu.make_async_remote_copy(
                src_ref=source, dst_ref=target, send_sem=e_send.at[e, way], recv_sem=e_recv.at[e, way],
                device_id=place(d_block, d_x), device_id_type=MESH)

        first, last = pl.ds(0, HALO), pl.ds(ROWS - HALO, HALO)
        own = pl.ds(HALO, ROWS)
        before, after = pl.ds(0, HALO), pl.ds(HALO + ROWS, HALO)
        rows = [
            copy(UP, volume.at[:, first, :], down.at[e], -1, 0),
            copy(DOWN, volume.at[:, last, :], up.at[e], 1, 0),
        ]
        for exists, _, _, c in rows:
            pl.when(exists)(c.start)

        @pl.loop(0, 4)
        def _(j):
            packed_left = jnp.zeros((ROWS, 128), F32)
            packed_right = jnp.zeros((ROWS, 128), F32)
            for g in range(8):
                ends = jnp.where(lane < 64, volume[4 * g + j, :, 0:128], volume[4 * g + j, :, 128:256])
                if g:
                    ends = pltpu.roll(ends, 16 * g, 1)
                packed_left = jnp.where(lane // 16 == g, ends, packed_left)
                packed_right = jnp.where(lane // 16 == (g + 7) % 8, ends, packed_right)
            send_left[e, j] = packed_left
            send_right[e, j] = packed_right

        sides = [
            copy(LEFT, send_left.at[e], right.at[e, :, own, :], 0, -1),
            copy(RIGHT, send_right.at[e], left.at[e, :, own, :], 0, 1),
            copy(LEFT_UP, send_left.at[e, :, first, :], right.at[e, :, after, :], -1, -1),
            copy(LEFT_DOWN, send_left.at[e, :, last, :], right.at[e, :, before, :], 1, -1),
            copy(RIGHT_UP, send_right.at[e, :, first, :], left.at[e, :, after, :], -1, 1),
            copy(RIGHT_DOWN, send_right.at[e, :, last, :], left.at[e, :, before, :], 1, 1),
        ]
        for exists, _, _, c in sides:
            pl.when(exists)(c.start)
        for _, comes, target, c in rows + sides:
            pl.when(comes)(c.wait_recv)
            @pl.when(jnp.logical_not(comes))
            def _():
                target[...] = jnp.zeros(target.shape, F32)
        return [(exists, c) for exists, _, _, c in rows + sides]

    def blur(e, way, volume, finish):
        down_band = (band_d[way, 0], band_d[way, 1])

        @pl.loop(0, 4)
        def _(j):
            values = jnp.concatenate([left[e, j], right[e, j]], axis=1)
            high, low = split(dot3(down_band, split(values)))
            start = pl.multiple_of(j * ROWS, ROWS)
            strips[0, pl.ds(start, ROWS), :] = high
            strips[1, pl.ds(start, ROWS), :] = low

        @pl.loop(0, 8)
        def _(g):
            parts = []
            for j in range(4):
                plane = 4 * g + j
                values = jnp.concatenate([up[e, plane], volume[plane], down[e, plane]], axis=0)
                parts.append(dot3(down_band, split(values)))
            own = split(jnp.concatenate(parts, axis=0))
            result = dot3(own, (band_w[way, 0], band_w[way, 1]))
            result += dot3((strips[0], strips[1]), (band_h[way, 0, g], band_h[way, 1, g]))
            mid[pl.ds(4 * g, 4)] = result.reshape(4, ROWS, COLS)

        axial = (band_a[way, 0], band_a[way, 1])

        def axial_rows(b):
            start = pl.multiple_of(8 * b, 8)
            where = pl.ds(start, 8)
            values = mid[:, where, :].reshape(256, COLS)
            finish(where, dot3(axial, split(values)).reshape(PLANES, 8, COLS))

        return axial_rows

    def to_quotient(where, blurred):
        quo[:, where, :] = data[:, where, :] / (blurred + BACKGROUND)

    def to_estimate(where, correction):
        est[:, where, :] = est[:, where, :] * correction

    for it in range(ITERS):
        sent_est = exchange(2 * it, est)
        forward = blur(2 * it, 0, est, to_quotient)
        if it:
            for exists, c in sent_quo:
                pl.when(exists)(c.wait_send)
        pl.loop(0, 8)(forward)
        sent_quo = exchange(2 * it + 1, quo)
        backward = blur(2 * it + 1, 1, quo, to_estimate)
        for exists, c in sent_est:
            pl.when(exists)(c.wait_send)
        if it < ITERS - 1:
            pl.loop(0, 8)(backward)

    pieces = []
    columns = pl.ds(pl.multiple_of(256 * x, 256), 256)
    for i in range(4):
        backward(2 * i)
        backward(2 * i + 1)
        owner = 4 * core + i
        source = est.at[:, pl.ds(16 * i, 16), :]
        target = out.at[:, :, columns]
        remote = pltpu.make_async_remote_copy(
            src_ref=source, dst_ref=target, send_sem=t_send.at[i], recv_sem=t_recv.at[x],
            device_id=(scan, owner), device_id_type=MESH)
        local = pltpu.make_async_copy(source, target, t_recv.at[x])
        pl.when(owner == row)(local.start)
        pl.when(owner != row)(remote.start)
        pieces.append((owner != row, remote))
    for i in range(4):
        target = out.at[:, :, pl.ds(256 * i, 256)]
        pltpu.make_async_copy(target, target, t_recv.at[i]).wait()

    for exists, c in pieces + sent_quo:
        pl.when(exists)(c.wait_send)
    for n in range(2):
        for k in range(WINDOW):
            for cb in range(4):
                _, _, is_remote, remote = deskew_copies(n, k, cb)
                pl.when(is_remote)(remote.wait_send)


def shards(raw_planes, shear_tiles, axial_kernel, column_kernel, row_kernel):
    raw = raw_planes.reshape(2, TILES, 16, 1024)
    taps = (axial_kernel, column_kernel, row_kernel)
    vmem = pl.BlockSpec(memory_space=pltpu.VMEM)
    smem = pl.BlockSpec(memory_space=pltpu.SMEM)
    half = (ITERS * 2, PLANES, HALO, COLS)
    strip = (ITERS * 2, 4, ROWS + 2 * HALO, 128)
    out = pl.pallas_call(
        body,
        out_shape=jax.ShapeDtypeStruct((PLANES, 16, 1024), F32),
        in_specs=[vmem, smem, smem, smem, smem, vmem, vmem, vmem],
        out_specs=pl.BlockSpec(memory_space=pl.ANY),
        scratch_shapes=[
            pltpu.VMEM((2, WINDOW, 16, 1024), F32),
            pltpu.VMEM((PLANES, ROWS, COLS), F32),
            pltpu.VMEM((PLANES, ROWS, COLS), F32),
            pltpu.VMEM((PLANES, ROWS, COLS), F32),
            pltpu.VMEM((PLANES, ROWS, COLS), F32),
            pltpu.VMEM(half, F32),
            pltpu.VMEM(half, F32),
            pltpu.VMEM(strip, F32),
            pltpu.VMEM(strip, F32),
            pltpu.VMEM((ITERS * 2, 4, ROWS, 128), F32),
            pltpu.VMEM((ITERS * 2, 4, ROWS, 128), F32),
            pltpu.VMEM((2, 2, ROWS, ROWS + 2 * HALO), BF16),
            pltpu.VMEM((2, 2, COLS, COLS), BF16),
            pltpu.VMEM((2, 2, 8, 256, COLS), BF16),
            pltpu.VMEM((2, 2, 256, 256), BF16),
            pltpu.VMEM((2, 4 * ROWS, 256), BF16),
            pltpu.SemaphoreType.DMA((2, WINDOW, 4)),
            pltpu.SemaphoreType.DMA((PLANES,)),
            pltpu.SemaphoreType.DMA((ITERS * 2, 8)),
            pltpu.SemaphoreType.DMA((ITERS * 2, 8)),
            pltpu.SemaphoreType.DMA((4,)),
            pltpu.SemaphoreType.DMA((4,)),
        ],
        compiler_params=pltpu.CompilerParams(has_side_effects=True, vmem_limit_bytes=48 << 20),
        name="deconvolve",
    )(raw, shear_tiles, *taps, *(t.reshape(1, -1) for t in taps))
    return out.reshape(PLANES, 1, 16, 1024)


def solution(mesh):
    return jax.shard_map(
        shards,
        mesh=mesh,
        in_specs=(P("scan", None, "row", None), P("scan"), P(), P(), P()),
        out_specs=P(None, "scan", "row", None),
        check_vma=False,
    )
```

time: 942 us -> 135 us (0.14)
  the two profiles are of different devices: /device:TPU:32 before, /device:TPU:33 now
where the time goes in v1:
time: 135 us
  Pallas kernels  130 us (96%)
  local copies, waits for them, and re-layouts  5.07 us (4%)
    pallas_call x1, Pallas kernels, shards(): pl.pallas_call(body, out_shape=jax.ShapeDtypeStruct((PLANES, 16, 1024), F...  130 us
    unnamed x11, local copies, waits for them, and re-layouts  5.07 us

profile of v1, /device:TPU:33, one launch (start us, length us, event | category | flops | bytes accessed | tf_op | source)
XLA Modules:
  0.0 135.2 jit_solution(9284357549214671691)
XLA Ops:
  0.0 0.0 copy-start
  0.0 1.1 copy-done
  1.1 0.0 copy-start.1
  1.1 0.7 copy-done.1
  1.8 0.0 copy-start.2
  1.8 0.7 copy-done.2
  2.4 0.0 copy-start.3
  2.4 0.7 copy-done.3
  3.1 0.0 copy-start.4
  3.1 0.7 copy-done.4
  3.8 130.1 %deconvolve.1 = f32[32,16,1024]{2,1,0:T(8,128)S(1)} custom-call(f32[2,6,16,1024]{3,2,1,0:T(8,128)S(1)} %copy-done, s32[2]{0:T(128)S(1)} %copy-done.4, f32[64]{0:T(128)S(1)} %copy-done.1, f32[31]{0:T(128)S(1)} %copy-done.2, f32[31]{0:T(128)S(1)} %copy-done.3, f32[1,64]{1,0:T(1,128)S(1)} %bitcast.7, f32[1,31]{1,0:T(1,128)S(1)} %bitcast.8, f32[1,31]{1,0:T(1,128)S(1)} %bitcast.9), custom_call_target="tpu_custom_call" | custom-call | tf_op jit(solution)/shard_map/deconvolve/pallas_call | solution.py:298
  133.8 1.3 copy.8
Async XLA Ops:
  0.0 1.1 copy-start
  1.1 0.7 copy-start.1
  1.8 0.7 copy-start.2
  2.4 0.7 copy-start.3
  3.1 0.7 copy-start.4

commit v2 on v1

v2 whole, which is shorter than its diff:
```python
import jax
import jax.numpy as jnp
from jax import lax
from jax.experimental import pallas as pl
from jax.experimental.pallas import tpu as pltpu
from jax.sharding import PartitionSpec as P

PLANES = 32
TILES = 6
WINDOW = 8
LAST_TILE = 10
ROWS = 64
COLS = 256
HALO = 16
ITERS = 2
BACKGROUND = 0.5
F32 = jnp.float32
BF16 = jnp.bfloat16
MESH = pl.DeviceIdType.MESH
UP, DOWN, LEFT, RIGHT, LEFT_UP, LEFT_DOWN, RIGHT_UP, RIGHT_DOWN = range(8)


def split(value):
    high = value.astype(BF16)
    low = (value - high.astype(F32)).astype(BF16)
    return high, low


def dot(a, b):
    return jnp.dot(a, b, preferred_element_type=F32)


def iota(shape, axis):
    return lax.broadcasted_iota(jnp.int32, shape, axis)


def pick(taps, count, index):
    value = jnp.zeros(index.shape, F32)
    for tap in range(count):
        value = jnp.where(index == tap, taps[tap], value)
    return value


def plane_base(plane):
    return (plane * 5) // 31


def body(raw_in, shear_in, ax_in, co_in, ro_in, out,
         raw, shear, ax_s, co_s, ro_s, win, data, est, quo, mid, up, down, left, right, send_left, send_right,
         band_d, band_w, band_a, masks, parts,
         in_sem, d_send, d_recv, e_send, e_recv, t_send, t_recv):
    scan = lax.axis_index("scan")
    row = lax.axis_index("row")
    x = row // 2
    core = row % 2
    block = 2 * scan + core
    half = x // 2

    loads = [pltpu.make_async_copy(a, b, in_sem.at[i]) for i, (a, b) in enumerate(
        [(shear_in, shear), (raw_in.at[0], raw.at[0]), (raw_in.at[1], raw.at[1]), (ax_in, ax_s), (co_in, co_s), (ro_in, ro_s)])]
    for load in loads:
        load.start()

    barrier = pltpu.get_barrier_semaphore()

    def inside(d_block, d_x):
        return jnp.logical_and(jnp.logical_and(block + d_block >= 0, block + d_block < 32),
                               jnp.logical_and(x + d_x >= 0, x + d_x < 4))

    def place(d_block, d_x):
        other = block + d_block
        return (other // 2, 2 * (x + d_x) + other % 2)

    def greet(condition, device):
        @pl.when(condition)
        def _():
            pl.semaphore_signal(barrier, inc=1, device_id=device, device_id_type=MESH)

    def window(source):
        first = plane_base(2 * source) - 1
        last = plane_base(2 * source + 1) + 6
        return jnp.maximum(first, 0), jnp.minimum(last, LAST_TILE)

    @pl.loop(0, 16)
    def _(source):
        first, last = window(source)
        sends = jnp.logical_and(scan >= first, scan <= last)
        for i in range(4):
            other = 4 * core + i
            greet(jnp.logical_and(sends, jnp.logical_or(source != scan, other != row)), (source, other))

    count = 0
    for d_block in (-1, 0, 1):
        for d_x in (-1, 0, 1):
            if d_block or d_x:
                greet(inside(d_block, d_x), place(d_block, d_x))
                count = count + inside(d_block, d_x).astype(jnp.int32)
    for i in range(4):
        other = 2 * i + row // 4
        greet(other != row, (scan, other))
    first, last = window(scan)
    count = count + 4 * (last - first + 1)
    to_self = jnp.logical_and(jnp.logical_and(scan >= first, scan <= last), half == core)
    count = count - to_self.astype(jnp.int32)
    count = count + 4 - (row // 4 == core).astype(jnp.int32)

    loads[0].wait()
    for n in range(2):
        loads[1 + n].wait()
        delta = shear[n] - plane_base(2 * scan + n)
        for k in range(WINDOW):
            zero = jnp.zeros(raw.shape[2:], F32)
            early = raw[n, k] if k < TILES else zero
            level = raw[n, k - 1] if 1 <= k <= TILES else zero
            late = raw[n, k - 2] if k >= 2 else zero
            win[n, k] = jnp.where(delta == 0, level, jnp.where(delta < 0, early, late))

    def deskew_copies(n, i, j):
        plane = 2 * scan + n
        k = (scan + i) % WINDOW
        cb = (x + j) % 4
        tile = plane_base(plane) - 1 + k
        offset = 32 * (x % 2) + 16 * core
        source = win.at[n, k, :, pl.ds(pl.multiple_of(256 * cb, 256), 256)]
        target = data.at[plane, pl.ds(pl.multiple_of(offset, 16), 16), :]
        real = jnp.logical_and(tile >= 0, tile <= LAST_TILE)
        mine = jnp.logical_and(tile == scan, jnp.logical_and(cb == x, half == core))
        remote = pltpu.make_async_remote_copy(
            src_ref=source, dst_ref=target, send_sem=d_send.at[n, i, j], recv_sem=d_recv.at[plane],
            device_id=(tile, 2 * cb + half), device_id_type=MESH)
        return jnp.logical_and(real, mine), (source, target, d_recv.at[plane]), jnp.logical_and(real, jnp.logical_not(mine)), remote

    pl.semaphore_wait(barrier, count)
    for n in range(2):
        for i in range(WINDOW):
            for j in range(4):
                is_local, local, is_remote, remote = deskew_copies(n, i, j)
                if j == 0:
                    @pl.when(is_local)
                    def _():
                        pltpu.make_async_copy(*local).start()
                pl.when(is_remote)(remote.start)

    for load in loads[3:]:
        load.wait()

    def total_of(taps, n):
        total = taps[0]
        for k in range(1, n):
            total = total + taps[k]
        return total

    ax_total, co_total, ro_total = total_of(ax_s, 64), total_of(co_s, 31), total_of(ro_s, 31)
    span = ROWS + 2 * HALO
    group = iota((16, 256), 1) // 16
    for g in range(8):
        masks[g] = jnp.where(group < 8, jnp.where(group == (g + 7) % 8, 1.0, 0.0), jnp.where(group == g + 8, 1.0, 0.0)).astype(BF16)
    for way in range(2):
        sign = 1 if way == 0 else -1
        shape = (ROWS, span)
        step = iota(shape, 1) - HALO - iota(shape, 0)
        high, low = split(pick(ro_s, 31, sign * step + 15) / ro_total)
        band_d[way] = jnp.concatenate([
            jnp.concatenate([high, high], axis=1), jnp.concatenate([low, jnp.zeros(shape, BF16)], axis=1)], axis=0)

        shape = (16, COLS)

        @pl.loop(0, 16)
        def _(b):
            start = pl.multiple_of(b * 16, 16)
            step = start + iota(shape, 0) - iota(shape, 1)
            high, low = split(pick(co_s, 31, sign * step + 15) / co_total)
            band_w[way, 0, pl.ds(start, 16), :] = high
            band_w[way, 1, pl.ds(start, 16), :] = low
        step = iota(shape, 0) - HALO - iota(shape, 1)
        left_band = split(pick(co_s, 31, sign * step + 15) / co_total)
        step = iota(shape, 0) + COLS - iota(shape, 1)
        right_band = split(pick(co_s, 31, sign * step + 15) / co_total)
        for part in range(2):
            for g in range(8):
                band_w[way, part, 256 + 16 * g:272 + 16 * g, :] = left_band[part]
                band_w[way, part, 384 + 16 * g:400 + 16 * g, :] = right_band[part]

        @pl.loop(0, 16)
        def _(b):
            start = pl.multiple_of(b * 16, 16)
            i = start + iota(shape, 0)
            j = iota(shape, 1)
            step = j // 8 - i // 8
            index = jnp.where(i % 8 == j % 8, sign * step + 32, -1)
            high, low = split(pick(ax_s, 64, index) / ax_total)
            band_a[way, pl.ds(start, 16), :] = jnp.concatenate([high, high, low], axis=1)

    first, last = pl.ds(0, HALO), pl.ds(ROWS - HALO, HALO)
    own = pl.ds(HALO, ROWS)
    before, after = pl.ds(0, HALO), pl.ds(HALO + ROWS, HALO)

    def row_copies(e, volume, planes):
        return [
            (UP, volume.at[planes, first, :], down.at[e, planes], -1, 0),
            (DOWN, volume.at[planes, last, :], up.at[e, planes], 1, 0),
        ]

    def side_copies(e, h):
        return [
            (LEFT, send_left.at[e, h], right.at[e, h, own, :], 0, -1),
            (RIGHT, send_right.at[e, h], left.at[e, h, own, :], 0, 1),
            (LEFT_UP, send_left.at[e, h, first, :], right.at[e, h, after, :], -1, -1),
            (LEFT_DOWN, send_left.at[e, h, last, :], right.at[e, h, before, :], 1, -1),
            (RIGHT_UP, send_right.at[e, h, first, :], left.at[e, h, after, :], -1, 1),
            (RIGHT_DOWN, send_right.at[e, h, last, :], left.at[e, h, before, :], 1, 1),
        ]

    def descriptor(e, h, way, source, target, d_block, d_x):
        return pltpu.make_async_remote_copy(
            src_ref=source, dst_ref=target, send_sem=e_send.at[e, way], recv_sem=e_recv.at[e, h, way],
            device_id=place(d_block, d_x), device_id_type=MESH)

    def chunk(h):
        return pl.ds(8 * h, 8)

    def start(e, h, copies):
        for c in copies:
            pl.when(inside(c[3], c[4]))(descriptor(e, h, *c).start)

    def arrive(e, h, volume):
        for c in row_copies(e, volume, chunk(h)) + side_copies(e, h):
            comes = inside(-c[3], -c[4])
            pl.when(comes)(descriptor(e, h, *c).wait_recv)
            @pl.when(jnp.logical_not(comes))
            def _():
                c[2][...] = jnp.zeros(c[2].shape, F32)

    def drain(e, volume):
        every = slice(None)
        for c in row_copies(e, volume, every) + side_copies(e, every):
            pl.when(inside(c[3], c[4]))(descriptor(e, 0, *c).wait_send)

    lane = iota((ROWS, 128), 1)

    def pack(e, h, volume):
        packed_left = jnp.zeros((ROWS, 128), F32)
        packed_right = jnp.zeros((ROWS, 128), F32)
        for g in range(8):
            ends = jnp.where(lane < 64, volume[8 * h + g, :, 0:128], volume[8 * h + g, :, 128:256])
            if g:
                ends = pltpu.roll(ends, 16 * g, 1)
            packed_left = jnp.where(lane // 16 == g, ends, packed_left)
            packed_right = jnp.where(lane // 16 == (g + 7) % 8, ends, packed_right)
        send_left[e, h] = packed_left
        send_right[e, h] = packed_right

    def along_rows(way, values):
        high, low = split(values)
        both = dot(band_d[way], jnp.concatenate([high, low], axis=0))
        return split(both[:ROWS] + both[ROWS:])

    def lateral(e, way, volume, h):
        strip = along_rows(way, jnp.concatenate([left[e, h], right[e, h]], axis=1))
        for g in range(8):
            plane = 8 * h + g
            high, low = along_rows(way, jnp.concatenate([up[e, plane], volume[plane], down[e, plane]], axis=0))
            here = pl.ds(ROWS * g, ROWS)
            parts[here, 0:256] = high
            parts[here, 256:512] = low
            for part in range(2):
                kept = strip[part].reshape(4, 16, 256) * masks[g][None]
                parts[here, 512 + 256 * part:768 + 256 * part] = kept.reshape(ROWS, 256)
        high, low = parts[:, 0:256], parts[:, 256:512]
        side_high, side_low = parts[:, 512:768], parts[:, 768:1024]
        values = jnp.concatenate([high, side_high, low, side_low, high, side_high], axis=1)
        bands = jnp.concatenate([band_w[way, 0], band_w[way, 0], band_w[way, 1]], axis=0)
        mid[chunk(h)] = dot(values, bands).reshape(8, ROWS, COLS)

    def axial(way, b):
        where = pl.ds(pl.multiple_of(8 * b, 8), 8)
        high, low = split(mid[:, where, :].reshape(256, COLS))
        value = dot(band_a[way], jnp.concatenate([high, low, high], axis=0)).reshape(PLANES, 8, COLS)
        if way == 0:
            quo[:, where, :] = data[:, where, :] / (value + BACKGROUND)
        else:
            est[:, where, :] = est[:, where, :] * value

    def axial_and_send(way, e, volume):
        @pl.loop(0, 4)
        def _(b):
            axial(way, b + 4 * (b // 2))

        @pl.loop(0, 4)
        def _(h):
            start(e, h, row_copies(e, volume, chunk(h)))

        @pl.loop(2, 6)
        def _(b):
            axial(way, b)

        @pl.loop(0, 4)
        def _(h):
            pack(e, h, volume)
            start(e, h, side_copies(e, h))

    def lateral_all(e, way, volume):
        @pl.loop(0, 4)
        def _(h):
            arrive(e, h, volume)
            lateral(e, way, volume, h)

    ring = scan // 4

    def turn(o):
        return (ring + o + o // 2 - 2 * (o // 3)) % 4

    @pl.loop(0, 5)
    def _(o):
        @pl.when(o < 4)
        def _():
            h = turn(o)
            for g in range(8):
                plane = 8 * h + g
                base = plane_base(plane)
                here = jnp.logical_and(jnp.logical_and(scan >= base - 1, scan <= base + 6), scan <= LAST_TILE)
                @pl.when(here)
                def _():
                    pltpu.make_async_copy(data.at[plane], data.at[plane], d_recv.at[plane]).wait()
                @pl.when(jnp.logical_not(here))
                def _():
                    data[plane] = jnp.zeros((ROWS, COLS), F32)
                est[plane] = data[plane] + 1.0
            start(0, h, row_copies(0, est, chunk(h)))
            pack(0, h, est)
            start(0, h, side_copies(0, h))

        @pl.when(o > 0)
        def _():
            h = turn(o - 1)
            arrive(0, h, est)
            lateral(0, 0, est, h)

    axial_and_send(0, 1, quo)
    lateral_all(1, 1, quo)
    drain(0, est)
    axial_and_send(1, 2, est)
    lateral_all(2, 0, est)
    drain(1, quo)
    axial_and_send(0, 3, quo)
    lateral_all(3, 1, quo)
    drain(2, est)

    pieces = []
    columns = pl.ds(pl.multiple_of(256 * x, 256), 256)
    for i in range(4):
        axial(1, 2 * i)
        axial(1, 2 * i + 1)
        owner = 4 * core + i
        source = est.at[:, pl.ds(16 * i, 16), :]
        target = out.at[:, :, columns]
        remote = pltpu.make_async_remote_copy(
            src_ref=source, dst_ref=target, send_sem=t_send.at[i], recv_sem=t_recv.at[x],
            device_id=(scan, owner), device_id_type=MESH)
        @pl.when(owner == row)
        def _():
            pltpu.make_async_copy(source, target, t_recv.at[x]).start()
        pl.when(owner != row)(remote.start)
        pieces.append((owner != row, remote))
    drain(3, quo)
    for n in range(2):
        for i in range(WINDOW):
            for j in range(4):
                _, _, is_remote, remote = deskew_copies(n, i, j)
                pl.when(is_remote)(remote.wait_send)
    for i in range(4):
        target = out.at[:, :, pl.ds(256 * i, 256)]
        pltpu.make_async_copy(target, target, t_recv.at[i]).wait()
    for exists, c in pieces:
        pl.when(exists)(c.wait_send)


def shards(raw_planes, shear_tiles, axial_kernel, column_kernel, row_kernel):
    raw = raw_planes.reshape(2, TILES, 16, 1024)
    hbm = pl.BlockSpec(memory_space=pltpu.HBM)
    half = (ITERS * 2, PLANES, HALO, COLS)
    strip = (ITERS * 2, 4, ROWS + 2 * HALO, 128)
    volume = pltpu.VMEM((PLANES, ROWS, COLS), F32)
    out = pl.pallas_call(
        body,
        out_shape=jax.ShapeDtypeStruct((PLANES, 16, 1024), F32),
        in_specs=[hbm] * 5,
        out_specs=pl.BlockSpec(memory_space=pl.ANY),
        scratch_shapes=[
            pltpu.VMEM((2, TILES, 16, 1024), F32),
            pltpu.SMEM((2,), jnp.int32),
            pltpu.SMEM((64,), F32),
            pltpu.SMEM((31,), F32),
            pltpu.SMEM((31,), F32),
            pltpu.VMEM((2, WINDOW, 16, 1024), F32),
            volume, volume, volume, volume,
            pltpu.VMEM(half, F32),
            pltpu.VMEM(half, F32),
            pltpu.VMEM(strip, F32),
            pltpu.VMEM(strip, F32),
            pltpu.VMEM((ITERS * 2, 4, ROWS, 128), F32),
            pltpu.VMEM((ITERS * 2, 4, ROWS, 128), F32),
            pltpu.VMEM((2, 2 * ROWS, 2 * (ROWS + 2 * HALO)), BF16),
            pltpu.VMEM((2, 2, 512, COLS), BF16),
            pltpu.VMEM((2, 256, 768), BF16),
            pltpu.VMEM((8, 16, 256), BF16),
            pltpu.VMEM((8 * ROWS, 1024), BF16),
            pltpu.SemaphoreType.DMA((6,)),
            pltpu.SemaphoreType.DMA((2, WINDOW, 4)),
            pltpu.SemaphoreType.DMA((PLANES,)),
            pltpu.SemaphoreType.DMA((ITERS * 2, 8)),
            pltpu.SemaphoreType.DMA((ITERS * 2, 4, 8)),
            pltpu.SemaphoreType.DMA((4,)),
            pltpu.SemaphoreType.DMA((4,)),
        ],
        compiler_params=pltpu.CompilerParams(collective_id=0, has_side_effects=True, vmem_limit_bytes=48 << 20),
        name="deconvolve",
    )(raw, shear_tiles, axial_kernel, column_kernel, row_kernel)
    return out.reshape(PLANES, 1, 16, 1024)


def solution(mesh):
    return jax.shard_map(
        shards,
        mesh=mesh,
        in_specs=(P("scan", None, "row", None), P("scan"), P(), P(), P()),
        out_specs=P(None, "scan", "row", None),
        check_vma=False,
    )
```

time: 135 us -> 122 us (0.904)
  the two profiles are of different devices: /device:TPU:33 before, /device:TPU:67 now
where the time goes in v2:
time: 122 us
  Pallas kernels  117 us (96%)
  local copies, waits for them, and re-layouts  5.07 us (4%)
    pallas_call x1, Pallas kernels, shards(): pl.pallas_call(body, out_shape=jax.ShapeDtypeStruct((PLANES, 16, 1024), F...  117 us
    unnamed x11, local copies, waits for them, and re-layouts  5.07 us

profile of v2, /device:TPU:67, one launch (start us, length us, event | category | flops | bytes accessed | tf_op | source)
XLA Modules:
  0.0 122.1 jit_solution(10092793550110563083)
XLA Ops:
  0.0 0.0 copy-start
  0.0 1.1 copy-done
  1.1 0.0 copy-start.1
  1.1 0.7 copy-done.1
  1.8 0.0 copy-start.2
  1.8 0.7 copy-done.2
  2.4 0.0 copy-start.3
  2.4 0.7 copy-done.3
  3.1 0.0 copy-start.4
  3.1 0.7 copy-done.4
  3.8 117.0 %deconvolve.1 = f32[32,16,1024]{2,1,0:T(8,128)S(1)} custom-call(f32[2,6,16,1024]{3,2,1,0:T(8,128)S(1)} %copy-done, s32[2]{0:T(128)S(1)} %copy-done.1, f32[64]{0:T(128)S(1)} %copy-done.2, f32[31]{0:T(128)S(1)} %copy-done.3, f32[31]{0:T(128)S(1)} %copy-done.4), custom_call_target="tpu_custom_call" | custom-call | tf_op jit(solution)/shard_map/deconvolve/pallas_call | solution.py:384
  120.8 1.3 %copy.8 = f32[32,1,16,1024]{3,2,1,0:T(8,128)} copy(f32[32,1,16,1024]{3,2,1,0:T(8,128)S(1)} %bitcast.3) | data formatting | bytes 4194304
Async XLA Ops:
  0.0 1.1 copy-start
  1.1 0.7 copy-start.1
  1.8 0.7 copy-start.2
  2.4 0.7 copy-start.3
  3.1 0.7 copy-start.4

commit v3 on v2

--- a/solution.py
+++ b/solution.py
@@ -55,6 +55,7 @@
     core = row % 2
     block = 2 * scan + core
     half = x // 2
+    ring = scan // 4
 
     loads = [pltpu.make_async_copy(a, b, in_sem.at[i]) for i, (a, b) in enumerate(
         [(shear_in, shear), (raw_in.at[0], raw.at[0]), (raw_in.at[1], raw.at[1]), (ax_in, ax_s), (co_in, co_s), (ro_in, ro_s)])]
@@ -117,13 +118,13 @@
 
     def deskew_copies(n, i, j):
         plane = 2 * scan + n
-        k = (scan + i) % WINDOW
+        base = plane_base(plane)
+        tile = 4 * ((1 + ring % 2 + i // 4) % 3) + (i + scan) % 4
         cb = (x + j) % 4
-        tile = plane_base(plane) - 1 + k
         offset = 32 * (x % 2) + 16 * core
-        source = win.at[n, k, :, pl.ds(pl.multiple_of(256 * cb, 256), 256)]
+        source = win.at[n, jnp.clip(tile - base + 1, 0, WINDOW - 1), :, pl.ds(pl.multiple_of(256 * cb, 256), 256)]
         target = data.at[plane, pl.ds(pl.multiple_of(offset, 16), 16), :]
-        real = jnp.logical_and(tile >= 0, tile <= LAST_TILE)
+        real = jnp.logical_and(jnp.logical_and(tile >= base - 1, tile <= base + 6), tile <= LAST_TILE)
         mine = jnp.logical_and(tile == scan, jnp.logical_and(cb == x, half == core))
         remote = pltpu.make_async_remote_copy(
             src_ref=source, dst_ref=target, send_sem=d_send.at[n, i, j], recv_sem=d_recv.at[plane],
@@ -131,8 +132,8 @@
         return jnp.logical_and(real, mine), (source, target, d_recv.at[plane]), jnp.logical_and(real, jnp.logical_not(mine)), remote
 
     pl.semaphore_wait(barrier, count)
-    for n in range(2):
-        for i in range(WINDOW):
+    for i in range(12):
+        for n in range(2):
             for j in range(4):
                 is_local, local, is_remote, remote = deskew_copies(n, i, j)
                 if j == 0:
@@ -270,109 +271,119 @@
         side_high, side_low = parts[:, 512:768], parts[:, 768:1024]
         values = jnp.concatenate([high, side_high, low, side_low, high, side_high], axis=1)
         bands = jnp.concatenate([band_w[way, 0], band_w[way, 0], band_w[way, 1]], axis=0)
-        mid[chunk(h)] = dot(values, bands).reshape(8, ROWS, COLS)
-
-    def axial(way, b):
-        where = pl.ds(pl.multiple_of(8 * b, 8), 8)
-        high, low = split(mid[:, where, :].reshape(256, COLS))
-        value = dot(band_a[way], jnp.concatenate([high, low, high], axis=0)).reshape(PLANES, 8, COLS)
-        if way == 0:
-            quo[:, where, :] = data[:, where, :] / (value + BACKGROUND)
-        else:
-            est[:, where, :] = est[:, where, :] * value
-
-    def axial_and_send(way, e, volume):
-        @pl.loop(0, 4)
-        def _(b):
-            axial(way, b + 4 * (b // 2))
+        return dot(values, bands).reshape(8, ROWS, COLS)
+
+    def axial(b):
+        where = pl.ds(8 * b, 8)
+
+        def product(way, value):
+            high, low = split(value)
+            return dot(band_a[way], jnp.concatenate([high, low, high], axis=0))
+
+        blurred = product(0, mid[:, where, :].reshape(256, COLS))
+        quotient = data[:, where, :].reshape(256, COLS) / (blurred + BACKGROUND)
+        quo[:, where, :] = product(1, quotient).reshape(PLANES, 8, COLS)
+
+    def axial_and_send(e):
+        for b in (0, 1, 6, 7):
+            axial(b)
 
         @pl.loop(0, 4)
         def _(h):
-            start(e, h, row_copies(e, volume, chunk(h)))
-
-        @pl.loop(2, 6)
-        def _(b):
-            axial(way, b)
+            start(e, h, row_copies(e, quo, chunk(h)))
+        for b in (2, 3, 4, 5):
+            axial(b)
 
         @pl.loop(0, 4)
         def _(h):
-            pack(e, h, volume)
+            pack(e, h, quo)
             start(e, h, side_copies(e, h))
 
-    def lateral_all(e, way, volume):
-        @pl.loop(0, 4)
-        def _(h):
-            arrive(e, h, volume)
-            lateral(e, way, volume, h)
-
-    ring = scan // 4
+    def send(e, h, volume):
+        start(e, h, row_copies(e, volume, chunk(h)))
+        pack(e, h, volume)
+        start(e, h, side_copies(e, h))
+
+    def forward(e, h):
+        arrive(e, h, est)
+        mid[chunk(h)] = lateral(e, 0, est, h)
+
+    def backward(e, h):
+        arrive(e, h, quo)
+        est[chunk(h)] = est[chunk(h)] * lateral(e, 1, quo, h)
 
     def turn(o):
         return (ring + o + o // 2 - 2 * (o // 3)) % 4
 
-    @pl.loop(0, 5)
+    @pl.loop(0, 4)
     def _(o):
-        @pl.when(o < 4)
-        def _():
-            h = turn(o)
-            for g in range(8):
-                plane = 8 * h + g
-                base = plane_base(plane)
-                here = jnp.logical_and(jnp.logical_and(scan >= base - 1, scan <= base + 6), scan <= LAST_TILE)
-                @pl.when(here)
-                def _():
-                    pltpu.make_async_copy(data.at[plane], data.at[plane], d_recv.at[plane]).wait()
-                @pl.when(jnp.logical_not(here))
-                def _():
-                    data[plane] = jnp.zeros((ROWS, COLS), F32)
-                est[plane] = data[plane] + 1.0
-            start(0, h, row_copies(0, est, chunk(h)))
-            pack(0, h, est)
-            start(0, h, side_copies(0, h))
-
-        @pl.when(o > 0)
-        def _():
-            h = turn(o - 1)
-            arrive(0, h, est)
-            lateral(0, 0, est, h)
-
-    axial_and_send(0, 1, quo)
-    lateral_all(1, 1, quo)
+        h = turn(o)
+        for g in range(8):
+            plane = 8 * h + g
+            base = plane_base(plane)
+            here = jnp.logical_and(jnp.logical_and(scan >= base - 1, scan <= base + 6), scan <= LAST_TILE)
+            @pl.when(here)
+            def _():
+                pltpu.make_async_copy(data.at[plane], data.at[plane], d_recv.at[plane]).wait()
+            @pl.when(jnp.logical_not(here))
+            def _():
+                data[plane] = jnp.zeros((ROWS, COLS), F32)
+            est[plane] = data[plane] + 1.0
+        send(0, h, est)
+
+    @pl.loop(0, 4)
+    def _(o):
+        forward(0, turn(o))
+
+    axial_and_send(1)
     drain(0, est)
-    axial_and_send(1, 2, est)
-    lateral_all(2, 0, est)
+
+    @pl.loop(0, 4)
+    def _(h):
+        backward(1, h)
+        send(2, h, est)
+
+    @pl.loop(0, 4)
+    def _(h):
+        forward(2, h)
+
     drain(1, quo)
-    axial_and_send(0, 3, quo)
-    lateral_all(3, 1, quo)
+    axial_and_send(3)
     drain(2, est)
 
-    pieces = []
     columns = pl.ds(pl.multiple_of(256 * x, 256), 256)
-    for i in range(4):
-        axial(1, 2 * i)
-        axial(1, 2 * i + 1)
+
+    def swap_copies(i, planes):
         owner = 4 * core + i
-        source = est.at[:, pl.ds(16 * i, 16), :]
-        target = out.at[:, :, columns]
+        source = est.at[planes, pl.ds(16 * i, 16), :]
+        target = out.at[planes, :, columns]
         remote = pltpu.make_async_remote_copy(
             src_ref=source, dst_ref=target, send_sem=t_send.at[i], recv_sem=t_recv.at[x],
             device_id=(scan, owner), device_id_type=MESH)
-        @pl.when(owner == row)
-        def _():
-            pltpu.make_async_copy(source, target, t_recv.at[x]).start()
-        pl.when(owner != row)(remote.start)
-        pieces.append((owner != row, remote))
+        return owner == row, (source, target, t_recv.at[x]), remote
+
+    @pl.loop(0, 4)
+    def _(h):
+        backward(3, h)
+        for i in range(4):
+            here, local, remote = swap_copies(i, chunk(h))
+            @pl.when(here)
+            def _():
+                pltpu.make_async_copy(*local).start()
+            pl.when(jnp.logical_not(here))(remote.start)
+
     drain(3, quo)
     for n in range(2):
-        for i in range(WINDOW):
+        for i in range(12):
             for j in range(4):
                 _, _, is_remote, remote = deskew_copies(n, i, j)
                 pl.when(is_remote)(remote.wait_send)
     for i in range(4):
         target = out.at[:, :, pl.ds(256 * i, 256)]
         pltpu.make_async_copy(target, target, t_recv.at[i]).wait()
-    for exists, c in pieces:
-        pl.when(exists)(c.wait_send)
+    for i in range(4):
+        here, _, remote = swap_copies(i, slice(None))
+        pl.when(jnp.logical_not(here))(remote.wait_send)
 
 
 def shards(raw_planes, shear_tiles, axial_kernel, column_kernel, row_kernel):
@@ -406,14 +417,14 @@
             pltpu.VMEM((8, 16, 256), BF16),
             pltpu.VMEM((8 * ROWS, 1024), BF16),
             pltpu.SemaphoreType.DMA((6,)),
-            pltpu.SemaphoreType.DMA((2, WINDOW, 4)),
+            pltpu.SemaphoreType.DMA((2, 12, 4)),
             pltpu.SemaphoreType.DMA((PLANES,)),
             pltpu.SemaphoreType.DMA((ITERS * 2, 8)),
             pltpu.SemaphoreType.DMA((ITERS * 2, 4, 8)),
             pltpu.SemaphoreType.DMA((4,)),
             pltpu.SemaphoreType.DMA((4,)),
         ],
-        compiler_params=pltpu.CompilerParams(collective_id=0, has_side_effects=True, vmem_limit_bytes=48 << 20),
+        compiler_params=pltpu.CompilerParams(collective_id=0, has_side_effects=True, vmem_limit_bytes=60 << 20),
         name="deconvolve",
     )(raw, shear_tiles, axial_kernel, column_kernel, row_kernel)
     return out.reshape(PLANES, 1, 16, 1024)

time: 122 us -> 103 us (0.84)
  the two profiles are of different devices: /device:TPU:67 before, /device:TPU:65 now
where the time goes in v3:
time: 103 us; the launch traced here: 102 us
  Pallas kernels  99.2 us (96%)
  local copies, waits for them, and re-layouts  3.16 us (3%)
    pallas_call x1, Pallas kernels, shards(): pl.pallas_call(body, out_shape=jax.ShapeDtypeStruct((PLANES, 16, 1024), F...  99.2 us
    unnamed x1, local copies, waits for them, and re-layouts  3.16 us

profile of v3, /device:TPU:65, one launch (start us, length us, event | category | flops | bytes accessed | tf_op | source)
XLA Modules:
  0.0 102.4 jit_solution(2235008631978864303)
XLA Ops:
  0.0 99.2 %deconvolve.1 = f32[32,16,1024]{2,1,0:T(8,128)} custom-call(f32[2,6,16,1024]{3,2,1,0:T(8,128)} %raw_in.1, s32[2]{0:T(128)} %shear_in.1, f32[64]{0:T(128)} %ax_in.1, f32[31]{0:T(128)} %co_in.1, f32[31]{0:T(128)} %ro_in.1), custom_call_target="tpu_custom_call" | custom-call | tf_op jit(solution)/shard_map/deconvolve/pallas_call | solution.py:395
  99.2 3.2 %copy.8 = f32[32,1,16,1024]{3,2,1,0:T(8,128)} copy(f32[32,1,16,1024]{3,2,1,0:T(8,128)} %bitcast.3) | data formatting | bytes 4194304

commit v4 on v3

--- a/solution.py
+++ b/solution.py
@@ -12,6 +12,7 @@
 ROWS = 64
 COLS = 256
 HALO = 16
+INSIDE = ROWS - 2 * HALO
 ITERS = 2
 BACKGROUND = 0.5
 F32 = jnp.float32
@@ -47,7 +48,7 @@
 
 def body(raw_in, shear_in, ax_in, co_in, ro_in, out,
          raw, shear, ax_s, co_s, ro_s, win, data, est, quo, mid, up, down, left, right, send_left, send_right,
-         band_d, band_w, band_a, masks, parts,
+         band_d, band_i, band_e, band_w, band_a, masks, parts,
          in_sem, d_send, d_recv, e_send, e_recv, t_send, t_recv):
     scan = lax.axis_index("scan")
     row = lax.axis_index("row")
@@ -132,7 +133,16 @@
         return jnp.logical_and(real, mine), (source, target, d_recv.at[plane]), jnp.logical_and(real, jnp.logical_not(mine)), remote
 
     pl.semaphore_wait(barrier, count)
+    def deskew_sent(items):
+        for i in items:
+            for n in range(2):
+                for j in range(4):
+                    _, _, is_remote, remote = deskew_copies(n, i, j)
+                    pl.when(is_remote)(remote.wait_send)
+
     for i in range(12):
+        if i == 8:
+            deskew_sent(range(4))
         for n in range(2):
             for j in range(4):
                 is_local, local, is_remote, remote = deskew_copies(n, i, j)
@@ -158,11 +168,16 @@
         masks[g] = jnp.where(group < 8, jnp.where(group == (g + 7) % 8, 1.0, 0.0), jnp.where(group == g + 8, 1.0, 0.0)).astype(BF16)
     for way in range(2):
         sign = 1 if way == 0 else -1
-        shape = (ROWS, span)
-        step = iota(shape, 1) - HALO - iota(shape, 0)
-        high, low = split(pick(ro_s, 31, sign * step + 15) / ro_total)
-        band_d[way] = jnp.concatenate([
-            jnp.concatenate([high, high], axis=1), jnp.concatenate([low, jnp.zeros(shape, BF16)], axis=1)], axis=0)
+        def rows_band(band, count, width, line):
+            shape = (count, width)
+            step = iota(shape, 1) - HALO - line(iota(shape, 0))
+            high, low = split(pick(ro_s, 31, sign * step + 15) / ro_total)
+            band[way] = jnp.concatenate([
+                jnp.concatenate([high, high], axis=1), jnp.concatenate([low, jnp.zeros(shape, BF16)], axis=1)], axis=0)
+
+        rows_band(band_d, ROWS, span, lambda i: i)
+        rows_band(band_i, INSIDE, ROWS, lambda i: i)
+        rows_band(band_e, INSIDE, span, lambda i: jnp.where(i < HALO, i, i + INSIDE))
 
         shape = (16, COLS)
 
@@ -224,8 +239,8 @@
         for c in copies:
             pl.when(inside(c[3], c[4]))(descriptor(e, h, *c).start)
 
-    def arrive(e, h, volume):
-        for c in row_copies(e, volume, chunk(h)) + side_copies(e, h):
+    def arrive(e, h, copies):
+        for c in copies:
             comes = inside(-c[3], -c[4])
             pl.when(comes)(descriptor(e, h, *c).wait_recv)
             @pl.when(jnp.logical_not(comes))
@@ -251,27 +266,36 @@
         send_left[e, h] = packed_left
         send_right[e, h] = packed_right
 
-    def along_rows(way, values):
+    def along_rows(band, values):
         high, low = split(values)
-        both = dot(band_d[way], jnp.concatenate([high, low], axis=0))
-        return split(both[:ROWS] + both[ROWS:])
-
-    def lateral(e, way, volume, h):
-        strip = along_rows(way, jnp.concatenate([left[e, h], right[e, h]], axis=1))
+        both = dot(band, jnp.concatenate([high, low], axis=0))
+        count = both.shape[0] // 2
+        return split(both[:count] + both[count:])
+
+    ALL, MIDDLE, EDGES = (band_d, ROWS, True), (band_i, INSIDE, False), (band_e, INSIDE, True)
+
+    def lateral(e, way, volume, h, kind):
+        band, count, halo = kind
+        strip_rows = slice(None) if halo else own
+        strip = along_rows(band[way], jnp.concatenate([left[e, h, strip_rows], right[e, h, strip_rows]], axis=1))
         for g in range(8):
             plane = 8 * h + g
-            high, low = along_rows(way, jnp.concatenate([up[e, plane], volume[plane], down[e, plane]], axis=0))
-            here = pl.ds(ROWS * g, ROWS)
+            values = volume[plane]
+            if halo:
+                values = jnp.concatenate([up[e, plane], values, down[e, plane]], axis=0)
+            high, low = along_rows(band[way], values)
+            here = pl.ds(count * g, count)
             parts[here, 0:256] = high
             parts[here, 256:512] = low
             for part in range(2):
-                kept = strip[part].reshape(4, 16, 256) * masks[g][None]
-                parts[here, 512 + 256 * part:768 + 256 * part] = kept.reshape(ROWS, 256)
-        high, low = parts[:, 0:256], parts[:, 256:512]
-        side_high, side_low = parts[:, 512:768], parts[:, 768:1024]
+                kept = strip[part].reshape(count // 16, 16, 256) * masks[g][None]
+                parts[here, 512 + 256 * part:768 + 256 * part] = kept.reshape(count, 256)
+        used = pl.ds(0, 8 * count)
+        high, low = parts[used, 0:256], parts[used, 256:512]
+        side_high, side_low = parts[used, 512:768], parts[used, 768:1024]
         values = jnp.concatenate([high, side_high, low, side_low, high, side_high], axis=1)
         bands = jnp.concatenate([band_w[way, 0], band_w[way, 0], band_w[way, 1]], axis=0)
-        return dot(values, bands).reshape(8, ROWS, COLS)
+        return dot(values, bands).reshape(8, count, COLS)
 
     def axial(b):
         where = pl.ds(8 * b, 8)
@@ -284,20 +308,24 @@
         quotient = data[:, where, :].reshape(256, COLS) / (blurred + BACKGROUND)
         quo[:, where, :] = product(1, quotient).reshape(PLANES, 8, COLS)
 
-    def axial_and_send(e):
+    middle = pl.ds(HALO, INSIDE)
+
+    def axial_and_send(e, rows_first):
+        def send_rows():
+            for h in range(4):
+                start(e, h, row_copies(e, quo, chunk(h)))
+
         for b in (0, 1, 6, 7):
             axial(b)
-
-        @pl.loop(0, 4)
-        def _(h):
-            start(e, h, row_copies(e, quo, chunk(h)))
+        if rows_first:
+            send_rows()
         for b in (2, 3, 4, 5):
             axial(b)
-
-        @pl.loop(0, 4)
-        def _(h):
+        for h in range(4):
             pack(e, h, quo)
             start(e, h, side_copies(e, h))
+        if not rows_first:
+            send_rows()
 
     def send(e, h, volume):
         start(e, h, row_copies(e, volume, chunk(h)))
@@ -305,12 +333,22 @@
         start(e, h, side_copies(e, h))
 
     def forward(e, h):
-        arrive(e, h, est)
-        mid[chunk(h)] = lateral(e, 0, est, h)
+        arrive(e, h, row_copies(e, est, chunk(h)) + side_copies(e, h))
+        mid[chunk(h)] = lateral(e, 0, est, h, ALL)
 
     def backward(e, h):
-        arrive(e, h, quo)
-        est[chunk(h)] = est[chunk(h)] * lateral(e, 1, quo, h)
+        arrive(e, h, row_copies(e, quo, chunk(h)) + side_copies(e, h))
+        est[chunk(h)] = est[chunk(h)] * lateral(e, 1, quo, h, ALL)
+
+    def backward_middle(e, h):
+        arrive(e, h, side_copies(e, h)[:2])
+        est[chunk(h), middle] = est[chunk(h), middle] * lateral(e, 1, quo, h, MIDDLE)
+
+    def backward_edges(e, h):
+        arrive(e, h, row_copies(e, quo, chunk(h)) + side_copies(e, h)[2:])
+        value = lateral(e, 1, quo, h, EDGES)
+        est[chunk(h), first] = est[chunk(h), first] * value[:, :HALO]
+        est[chunk(h), last] = est[chunk(h), last] * value[:, HALO:]
 
     def turn(o):
         return (ring + o + o // 2 - 2 * (o // 3)) % 4
@@ -335,7 +373,7 @@
     def _(o):
         forward(0, turn(o))
 
-    axial_and_send(1)
+    axial_and_send(1, True)
     drain(0, est)
 
     @pl.loop(0, 4)
@@ -348,7 +386,7 @@
         forward(2, h)
 
     drain(1, quo)
-    axial_and_send(3)
+    axial_and_send(3, False)
     drain(2, est)
 
     columns = pl.ds(pl.multiple_of(256 * x, 256), 256)
@@ -362,22 +400,26 @@
             device_id=(scan, owner), device_id_type=MESH)
         return owner == row, (source, target, t_recv.at[x]), remote
 
-    @pl.loop(0, 4)
-    def _(h):
-        backward(3, h)
-        for i in range(4):
+    def swap(h, pieces):
+        for i in pieces:
             here, local, remote = swap_copies(i, chunk(h))
             @pl.when(here)
             def _():
                 pltpu.make_async_copy(*local).start()
             pl.when(jnp.logical_not(here))(remote.start)
 
+    @pl.loop(0, 4)
+    def _(h):
+        backward_middle(3, h)
+        swap(h, (1, 2))
+
+    @pl.loop(0, 4)
+    def _(h):
+        backward_edges(3, h)
+        swap(h, (0, 3))
+
     drain(3, quo)
-    for n in range(2):
-        for i in range(12):
-            for j in range(4):
-                _, _, is_remote, remote = deskew_copies(n, i, j)
-                pl.when(is_remote)(remote.wait_send)
+    deskew_sent(range(4, 12))
     for i in range(4):
         target = out.at[:, :, pl.ds(256 * i, 256)]
         pltpu.make_async_copy(target, target, t_recv.at[i]).wait()
@@ -388,6 +430,7 @@
 
 def shards(raw_planes, shear_tiles, axial_kernel, column_kernel, row_kernel):
     raw = raw_planes.reshape(2, TILES, 16, 1024)
+    operands = (raw, shear_tiles, axial_kernel, column_kernel, row_kernel)
     hbm = pl.BlockSpec(memory_space=pltpu.HBM)
     half = (ITERS * 2, PLANES, HALO, COLS)
     strip = (ITERS * 2, 4, ROWS + 2 * HALO, 128)
@@ -412,6 +455,8 @@
             pltpu.VMEM((ITERS * 2, 4, ROWS, 128), F32),
             pltpu.VMEM((ITERS * 2, 4, ROWS, 128), F32),
             pltpu.VMEM((2, 2 * ROWS, 2 * (ROWS + 2 * HALO)), BF16),
+            pltpu.VMEM((2, 2 * INSIDE, 2 * ROWS), BF16),
+            pltpu.VMEM((2, 2 * INSIDE, 2 * (ROWS + 2 * HALO)), BF16),
             pltpu.VMEM((2, 2, 512, COLS), BF16),
             pltpu.VMEM((2, 256, 768), BF16),
             pltpu.VMEM((8, 16, 256), BF16),
@@ -424,9 +469,9 @@
             pltpu.SemaphoreType.DMA((4,)),
             pltpu.SemaphoreType.DMA((4,)),
         ],
-        compiler_params=pltpu.CompilerParams(collective_id=0, has_side_effects=True, vmem_limit_bytes=60 << 20),
+        compiler_params=pltpu.CompilerParams(collective_id=0, has_side_effects=True, vmem_limit_bytes=48 << 20),
         name="deconvolve",
-    )(raw, shear_tiles, axial_kernel, column_kernel, row_kernel)
+    )(*(pltpu.with_memory_space_constraint(a, pltpu.HBM) for a in operands))
     return out.reshape(PLANES, 1, 16, 1024)
 
 

time: 103 us -> 96.9 us (0.941)
  the two profiles are of different devices: /device:TPU:65 before, /device:TPU:32 now
where the time goes in v4:
time: 96.9 us; the launch traced here: 96.8 us
  Pallas kernels  95.4 us (98%)
  local copies, waits for them, and re-layouts  1.32 us (1%)
    pallas_call x1, Pallas kernels, shards(): pl.pallas_call(body, out_shape=jax.ShapeDtypeStruct((PLANES, 16, 1024), F...  95.4 us

profile of v4, /device:TPU:32, one launch (start us, length us, event | category | flops | bytes accessed | tf_op | source)
XLA Modules:
  0.0 96.8 jit_solution(15754823786297002254)
XLA Ops:
  0.0 95.4 %deconvolve.1 = f32[32,16,1024]{2,1,0:T(8,128)S(1)} custom-call(f32[2,6,16,1024]{3,2,1,0:T(8,128)} %raw_in.1, s32[2]{0:T(128)} %shear_in.1, f32[64]{0:T(128)} %ax_in.1, f32[31]{0:T(128)} %co_in.1, f32[31]{0:T(128)} %ro_in.1), custom_call_target="tpu_custom_call" | custom-call | tf_op jit(solution)/shard_map/deconvolve/pallas_call | solution.py:438
  95.5 1.3 %copy.8 = f32[32,1,16,1024]{3,2,1,0:T(8,128)} copy(f32[32,1,16,1024]{3,2,1,0:T(8,128)S(1)} %bitcast.3) | data formatting | bytes 4194304

commit v5 on v4

--- a/solution.py
+++ b/solution.py
@@ -142,7 +142,7 @@
 
     for i in range(12):
         if i == 8:
-            deskew_sent(range(4))
+            deskew_sent(range(2))
         for n in range(2):
             for j in range(4):
                 is_local, local, is_remote, remote = deskew_copies(n, i, j)
@@ -270,7 +270,7 @@
         high, low = split(values)
         both = dot(band, jnp.concatenate([high, low], axis=0))
         count = both.shape[0] // 2
-        return split(both[:count] + both[count:])
+        return both[:count] + both[count:]
 
     ALL, MIDDLE, EDGES = (band_d, ROWS, True), (band_i, INSIDE, False), (band_e, INSIDE, True)
 
@@ -278,23 +278,28 @@
         band, count, halo = kind
         strip_rows = slice(None) if halo else own
         strip = along_rows(band[way], jnp.concatenate([left[e, h, strip_rows], right[e, h, strip_rows]], axis=1))
+        side_high = strip.astype(BF16).reshape(count // 16, 16, 256)
+        rest = strip - strip.astype(BF16).astype(F32)
+        rest = jnp.concatenate([pltpu.roll(rest[:, :128], 16, 1), pltpu.roll(rest[:, 128:], 16, 1)], axis=1)
+        side_low = rest.astype(BF16).reshape(count // 16, 16, 256)
         for g in range(8):
             plane = 8 * h + g
             values = volume[plane]
             if halo:
                 values = jnp.concatenate([up[e, plane], values, down[e, plane]], axis=0)
-            high, low = along_rows(band[way], values)
+            high, low = split(along_rows(band[way], values))
             here = pl.ds(count * g, count)
             parts[here, 0:256] = high
             parts[here, 256:512] = low
-            for part in range(2):
-                kept = strip[part].reshape(count // 16, 16, 256) * masks[g][None]
-                parts[here, 512 + 256 * part:768 + 256 * part] = kept.reshape(count, 256)
+            kept = side_high * masks[g][None]
+            both = kept + side_low * masks[(g + 1) % 8][None]
+            parts[here, 512:768] = kept.reshape(count, 256)
+            parts[here, 768:1024] = both.reshape(count, 256)
         used = pl.ds(0, 8 * count)
         high, low = parts[used, 0:256], parts[used, 256:512]
-        side_high, side_low = parts[used, 512:768], parts[used, 768:1024]
-        values = jnp.concatenate([high, side_high, low, side_low, high, side_high], axis=1)
-        bands = jnp.concatenate([band_w[way, 0], band_w[way, 0], band_w[way, 1]], axis=0)
+        side_high, side_both = parts[used, 512:768], parts[used, 768:1024]
+        values = jnp.concatenate([low, high, side_both, high, side_high], axis=1)
+        bands = jnp.concatenate([band_w[way, 0, 0:COLS, :], band_w[way, 0], band_w[way, 1]], axis=0)
         return dot(values, bands).reshape(8, count, COLS)
 
     def axial(b):
@@ -419,7 +424,7 @@
         swap(h, (0, 3))
 
     drain(3, quo)
-    deskew_sent(range(4, 12))
+    deskew_sent(range(2, 12))
     for i in range(4):
         target = out.at[:, :, pl.ds(256 * i, 256)]
         pltpu.make_async_copy(target, target, t_recv.at[i]).wait()

time: 96.9 us -> 96.3 us (level)
  no operation moved by 1% of the time
where the time goes in v5:
time: 96.3 us; the launch traced here: 96.1 us
  Pallas kernels  94.8 us (98%)
  local copies, waits for them, and re-layouts  1.32 us (1%)
    pallas_call x1, Pallas kernels, shards(): pl.pallas_call(body, out_shape=jax.ShapeDtypeStruct((PLANES, 16, 1024), F...  94.8 us

profile of v5, /device:TPU:32, one launch (start us, length us, event | category | flops | bytes accessed | tf_op | source)
XLA Modules:
  0.0 96.1 jit_solution(9667096271351565876)
XLA Ops:
  0.0 94.8 %deconvolve.1 = f32[32,16,1024]{2,1,0:T(8,128)S(1)} custom-call(f32[2,6,16,1024]{3,2,1,0:T(8,128)} %raw_in.1, s32[2]{0:T(128)} %shear_in.1, f32[64]{0:T(128)} %ax_in.1, f32[31]{0:T(128)} %co_in.1, f32[31]{0:T(128)} %ro_in.1), custom_call_target="tpu_custom_call" | custom-call | tf_op jit(solution)/shard_map/deconvolve/pallas_call | solution.py:443
  94.8 1.3 %copy.8 = f32[32,1,16,1024]{3,2,1,0:T(8,128)} copy(f32[32,1,16,1024]{3,2,1,0:T(8,128)S(1)} %bitcast.3) | data formatting | bytes 4194304
